TPU v7x, 32 devices: a whole 2x2x4 slice. The times are simulated.
32 devices in a mesh: groups: 2 (over x), ctx: 16 (over z, y, core).
Axes of the slice: x: 2, y: 2, z: 4, core: 2. Of those that a mesh axis runs over, the one named last changes fastest.
Arguments:
- conv_input: bfloat16 [4096, 5120], P(('groups', 'ctx')), parts along dimension 0, may hold values from -6 to 6
- step_raw: float32 [4096, 64], P(('groups', 'ctx')), parts along dimension 0, may hold values from -5 to 5.5
- step_bias: float32 [64], replicated, may hold values from -14 to -2
- decay_log: float32 [64], replicated, may hold values from -3 to 0.7
- skip_gain: float32 [64], replicated, may hold values from 0.5 to 1.5
- conv_weight: float32 [4, 5120], replicated, may hold values from -3 to 3
- conv_bias: float32 [5120], replicated, may hold values from -1 to 0.5
- doc_lengths: int32 [8], P('groups'), parts along dimension 0, may hold values from 1 to 1024, 2048 in all
- grad_out: bfloat16 [4096, 4096], P(('groups', 'ctx')), parts along dimension 0, may hold values from -400 to 400
Outputs:
- mixer_out: bfloat16 [4096, 4096], P(('groups', 'ctx')), parts along dimension 0
- grad_input: bfloat16 [4096, 5120], P(('groups', 'ctx')), parts along dimension 0
- grad_step: float32 [4096, 64], P(('groups', 'ctx')), parts along dimension 0
- grad_conv: float32 [10, 5120], P('groups'), parts along dimension 0
- grad_heads: float32 [6, 64], P('groups'), parts along dimension 0
There are 2 independent parts, one for each index of `groups`. A program takes and returns all parts, laid end to end along the dimension named above; an argument that names none is the same for every part. Nothing has to cross between parts.
Inputs may be any that keep to these rules, and one draw needn't show every extreme that they name: doc_lengths lists the lengths of the 4 documents that follow one another from token 0; they sum to 2048, and the longest has exactly 1024 tokens.
All inputs are finite; a program needn't handle non-finite values.
Results may differ from a plain program's by a relative error of at most 0.001.
Values may be sent and summed in bfloat16 or wider, within the bound.
No kernel may reach another device: no remote copies, remote signals or barrier semaphores. Data moves between devices by JAX's collectives and lax.ppermute only.
A program may use at most 192 MiB of HBM per device.

v0:
```python
from functools import partial
import math
import jax
import jax.numpy as jnp
from jax import lax
from jax.sharding import PartitionSpec as P

GROUPS = 4
HIGH = lax.Precision.HIGHEST


def passed_along(value, axis, steps):
    count = lax.axis_size(axis)
    initial, last = (max(0, -steps), min(count, count - steps))
    return lax.ppermute(value, axis, [(source, source + steps) for source in range(initial, last)])


def doc_offsets(doc_lengths, positions):
    ends = jnp.cumsum(doc_lengths, dtype=jnp.int32)
    starts = ends - doc_lengths
    before = starts[None, :] <= positions[:, None]
    opening = jnp.max(jnp.where(before, starts[None, :], 0), axis=1)
    return positions - opening


def convolve(extended, conv_weight, conv_bias, inside):
    count = inside.shape[0]
    taps = conv_weight.shape[0]
    total = jnp.zeros((count, extended.shape[1]), jnp.float32) + conv_bias[None, :]
    for lag in range(taps):
        reach = taps - 1 - lag
        valid = (inside >= reach).astype(jnp.float32)[:, None]
        total = total + conv_weight[lag][None, :] * extended[lag : lag + count] * valid
    return jax.nn.silu(total)


def prepare(
    extended, step_raw, step_bias, decay_log, skip_gain, conv_weight, conv_bias, inside, layout
):
    groups, headdim, block = layout
    length, heads = step_raw.shape
    share = heads // groups
    count = length // block
    inner = heads * headdim
    act = convolve(extended, conv_weight, conv_bias, inside)
    width = (act.shape[1] - inner) // 2
    inputs = act[:, :inner].reshape(count, block, groups, share, headdim)
    b_values = act[:, inner : inner + width].reshape(count, block, groups, width // groups)
    c_values = act[:, inner + width :].reshape(count, block, groups, width // groups)
    step_size = jax.nn.softplus(step_raw + step_bias[None, :])
    log_rate = (-step_size * jnp.exp(decay_log)[None, :]).reshape(count, block, groups, share)
    cum_decay = jnp.cumsum(log_rate, axis=1)
    return (
        inputs,
        b_values,
        c_values,
        step_size.reshape(count, block, groups, share),
        cum_decay,
        skip_gain.reshape(groups, share),
    )


def state_part(inputs, b_values, step_size, cum_decay, doc_count):
    whole = jnp.exp(cum_decay[:, -1]) * (doc_count[:, -1] == 0)[:, None, None]
    tail = (
        jnp.exp(cum_decay[:, -1:] - cum_decay) * (doc_count == doc_count[:, -1:])[:, :, None, None]
    )
    local = jnp.einsum(
        "cqgrp,cqgn->cgrpn", inputs * (tail * step_size)[..., None], b_values, precision=HIGH
    )

    def carry_step(carried, pieces):
        scale, state = carried
        factor, piece = pieces
        return ((factor * scale, factor[..., None, None] * state + piece), (scale, state))

    initial = (jnp.ones(whole.shape[1:], jnp.float32), jnp.zeros(local.shape[1:], jnp.float32))
    final, chains = lax.scan(carry_step, initial, (whole, local))
    return (final[0], final[1], chains[0], chains[1])


def out_part(
    inputs, b_values, c_values, step_size, cum_decay, skip_heads, a_chain, b_chain, doc_count
):
    block = doc_count.shape[1]
    order = jnp.arange(block, dtype=jnp.int32)
    allowed = (doc_count[:, :, None] == doc_count[:, None, :]) & (order[:, None] >= order[None, :])[
        None
    ]
    by_head = jnp.moveaxis(cum_decay, 1, -1)
    spread = by_head[..., :, None] - by_head[..., None, :]
    decay = jnp.exp(jnp.where(allowed[:, None, None], spread, -1e30))
    scores = jnp.einsum("ctgn,csgn->cgts", c_values, b_values, precision=HIGH)
    weights = scores[:, :, None] * decay * jnp.moveaxis(step_size, 1, -1)[..., None, :]
    y_diag = jnp.einsum("cgrts,csgrp->ctgrp", weights, inputs, precision=HIGH)
    head_in = jnp.exp(cum_decay) * (doc_count == 0)[:, :, None, None]
    y_carry = head_in[..., None] * jnp.einsum(
        "ctgn,cgrpn->ctgrp", c_values, b_chain, precision=HIGH
    )
    mixed = y_diag + y_carry + skip_heads[None, None, :, :, None] * inputs
    return (mixed, head_in * a_chain[:, None])


def outer_part(c_values, head_reach, state_in):
    return head_reach[..., None] * jnp.einsum(
        "ctgn,grpn->ctgrp", c_values, state_in, precision=HIGH
    )


def owner_join(earlier, later):
    factor_early, value_early = earlier
    factor_late, value_late = later
    return (factor_late * factor_early, factor_late * value_early + value_late)


def owner_prefix(pieces, reverse):
    values, factors = pieces
    scales, totals = lax.associative_scan(owner_join, (factors, values), reverse=reverse, axis=1)
    blank = jnp.zeros_like(totals[:, :1])
    if reverse:
        return jnp.concatenate([totals[:, 1:], blank], axis=1)
    return jnp.concatenate([blank, totals[:, :-1]], axis=1)


def body(
    conv_input,
    step_raw,
    step_bias,
    decay_log,
    skip_gain,
    conv_weight,
    conv_bias,
    doc_lengths,
    grad_out,
):
    length, feature_lanes = conv_input.shape
    heads = step_raw.shape[1]
    taps = conv_weight.shape[0]
    inner = grad_out.shape[1]
    headdim = inner // heads
    groups = GROUPS
    devices = lax.axis_size("ctx")
    block = math.gcd(length, 64)
    count = length // block
    border = length - taps + 1
    rim_rows = passed_along(conv_input[border:], "ctx", 1)
    extended = jnp.concatenate([rim_rows, conv_input], axis=0).astype(jnp.float32)
    positions = lax.axis_index("ctx") * length + jnp.arange(length, dtype=jnp.int32)
    inside = doc_offsets(doc_lengths, positions)
    doc_count = jnp.cumsum((inside == 0).astype(jnp.float32).reshape(count, block), axis=1)
    layout = (groups, headdim, block)
    prepared, prep_pull = jax.vjp(
        partial(prepare, inside=inside, layout=layout),
        extended,
        step_raw,
        step_bias,
        decay_log,
        skip_gain,
        conv_weight,
        conv_bias,
    )
    inputs, b_values, c_values, step_size, cum_decay, skip_heads = prepared
    summary, state_pull = jax.vjp(
        partial(state_part, doc_count=doc_count), inputs, b_values, step_size, cum_decay
    )
    decay_all, state_all, a_chain, b_chain = summary
    local_out, out_pull = jax.vjp(
        partial(out_part, doc_count=doc_count),
        inputs,
        b_values,
        c_values,
        step_size,
        cum_decay,
        skip_heads,
        a_chain,
        b_chain,
    )
    y_local, head_reach = local_out
    rates = jnp.broadcast_to(decay_all.reshape(heads, 1, 1), (heads, devices, 1))
    flat_states = state_all.reshape(heads, devices, -1)
    ready = owner_prefix(
        (
            lax.all_to_all(flat_states, "ctx", split_axis=1, concat_axis=1, tiled=True),
            lax.all_to_all(rates, "ctx", split_axis=1, concat_axis=1, tiled=True),
        ),
        False,
    )
    state_in = lax.all_to_all(ready, "ctx", split_axis=1, concat_axis=1, tiled=True).reshape(
        state_all.shape
    )
    y_state, exterior_vjp_fn = jax.vjp(outer_part, c_values, head_reach, state_in)
    mixer_out = (y_local + y_state).reshape(length, inner).astype(jnp.bfloat16)
    upstream = grad_out.astype(jnp.float32).reshape(y_local.shape)
    grad_c_outer, grad_reach, incoming_state_gradient = exterior_vjp_fn(upstream)
    pulled_out = out_pull((upstream, grad_reach))
    grad_inputs, grad_b, grad_c, grad_steps, grad_cum, grad_skip, grad_a_chain, grad_b_chain = (
        pulled_out
    )
    flat_grads = incoming_state_gradient.reshape(heads, devices, -1)
    ready = owner_prefix(
        (
            lax.all_to_all(flat_grads, "ctx", split_axis=1, concat_axis=1, tiled=True),
            lax.all_to_all(rates, "ctx", split_axis=1, concat_axis=1, tiled=True),
        ),
        True,
    )
    adjoint = lax.all_to_all(ready, "ctx", split_axis=1, concat_axis=1, tiled=True).reshape(
        state_all.shape
    )
    grad_decay_all = jnp.sum(adjoint * state_in, axis=(2, 3))
    grad_inputs_two, grad_b_two, grad_steps_two, grad_cum_two = state_pull(
        (grad_decay_all, adjoint, grad_a_chain, grad_b_chain)
    )
    pulled = prep_pull(
        (
            grad_inputs + grad_inputs_two,
            grad_b + grad_b_two,
            grad_c + grad_c_outer,
            grad_steps + grad_steps_two,
            grad_cum + grad_cum_two,
            grad_skip,
        )
    )
    grad_extended, grad_step, grad_bias, grad_log, grad_gain, grad_kernel, grad_kernel_bias = pulled
    returned = passed_along(grad_extended[: taps - 1], "ctx", -1)
    own_rows = grad_extended[taps - 1 :]
    grad_input = jnp.concatenate([own_rows[:border], own_rows[border:] + returned], axis=0).astype(
        jnp.bfloat16
    )
    totals = lax.psum(
        (
            jnp.concatenate([grad_kernel, grad_kernel_bias[None, :]], axis=0),
            jnp.stack([grad_bias, grad_log, grad_gain]),
        ),
        "ctx",
    )
    scale = (length * devices) ** (-0.5)
    return (mixer_out, grad_input, grad_step, totals[0] * scale, totals[1] * scale)


def solution(mesh):
    placed = (
        P(("groups", "ctx"), None),
        P(("groups", "ctx"), None),
        P(),
        P(),
        P(),
        P(),
        P(),
        P("groups"),
        P(("groups", "ctx"), None),
    )
    return jax.shard_map(
        body,
        mesh=mesh,
        in_specs=placed,
        out_specs=(
            P(("groups", "ctx"), None),
            P(("groups", "ctx"), None),
            P(("groups", "ctx"), None),
            P("groups", None),
            P("groups", None),
        ),
        check_vma=False,
    )
```

profile of v0, /device:TPU:8, one launch (start us, length us, event | category | flops | bytes accessed | tf_op | source)
XLA Modules:
  0.0 590.7 jit_solution(1007790423436295223)
XLA Ops:
  19.5 3.2 fusion.41
  25.8 4.7 reshape.284
  30.4 5.8 copy.292
  37.3 7.0 %fusion.35 = f32[2,4,16,64,128]{4,3,2,1,0:T(8,128)} fusion(f32[2,64,4,16,64]{1,4,3,2,0:T(8,128)} %copy.292, f32[2,64,4,16]{1,3,2,0:T(8,128)S(1)} %copy_multiply_fusion, f32[2,64,4,128,1]{3,2,1,0,4:T(4,128)S(1)} %bitcast.262), kind=kOutput, calls=%fused_computation.60 | convolution fusion | flops 805830656 | bytes 6586368 | tf_op jit(solution)/shard_map/jvp(cqgrp,cqgn->cgrpn)/dot_general | solution.py:68
  46.8 6.6 %while.40 = (s32[]{:T(128)}, f32[4,16]{1,0:T(4,128)S(1)}, f32[4,16,64,128]{3,2,1,0:T(8,128)S(1)}, f32[2,4,16]{2,1,0:T(4,128)S(1)}, f32[2,4,16,64,128]{4,3,2,1,0:...) while((s32[]{:T(128)}, f32[4,16]{1,0:T(4,128)S(1)}, ...), condition=%wide.region_5.6_spmd.clone, body=%wide.region_4.5_spmd.clone.sunk | while | flops 2097347 | bytes 27272616 | solution.py:78
  54.1 6.6 %all-to-all-start.1 = ((f32[64,16,1]{0,2,1:T(1,128)}), f32[64,16,1]{0,2,1:T(1,128)S(1)}, u32[]{:S(2)}, u32[]{:S(2)}) async-start(f32[64,16,1]{0,2,1:T(1,128)} %broadcast_in_dim.115), calls=%async_computation.1 | async-start | bytes 16384 | tf_op jit(solution)/shard_map/all_to_all | solution.py:184
  62.3 4.2 copy.300
  66.4 6.6 %all-to-all-start = ((f32[64,16,512]{2,0,1:T(8,128)}), f32[64,16,512]{2,0,1:T(8,128)S(1)}, u32[]{:S(2)}, u32[]{:S(2)}) async-start(f32[64,16,512]{2,0,1:T(8,128)} %copy.300), calls=%async_computation | async-start | bytes 4194304 | tf_op jit(solution)/shard_map/all_to_all | solution.py:183
  75.4 43.4 %all-to-all-done = f32[64,16,512]{2,0,1:T(8,128)S(1)} async-done(((f32[64,16,512]{2,0,1:T(8,128)}), f32[64,16,512]{2,0,1:T(8,128)S(1)}, u32[]{:S(2)}, u32[]{:S(2)}) %all-to-all-start) | async-done | bytes 2097184 | tf_op jit(solution)/shard_map/all_to_all | solution.py:183
  130.8 4.1 pad.96
  136.7 4.1 pad.95
  144.1 4.1 pad.143
  148.1 3.9 pad.221
  155.5 6.4 %all-to-all-start.2 = ((f32[64,16,512]{2,0,1:T(8,128)}), f32[64,16,512]{2,0,1:T(8,128)S(1)}, u32[]{:S(2)}, u32[]{:S(2)}) async-start(f32[64,16,512]{2,0,1:T(8,128)} %concatenate.38), calls=%async_computation.2 | async-start | bytes 4194304 | tf_op jit(solution)/shard_map/all_to_all | solution.py:188
  161.9 3.3 reshape.291
  165.3 5.9 %copy.305 = f32[2,64,4,16,64]{1,4,3,2,0:T(8,128)} copy(f32[2,64,4,16,64]{4,3,2,1,0:T(8,128)} %reshape.291) | data formatting | bytes 4194304 | tf_op jit(solution)/shard_map/reshape | solution.py:193
  171.3 36.5 %all-to-all-done.2 = f32[64,16,512]{2,0,1:T(8,128)S(1)} async-done(((f32[64,16,512]{2,0,1:T(8,128)}), f32[64,16,512]{2,0,1:T(8,128)S(1)}, u32[]{:S(2)}, u32[]{:S(2)}) %all-to-all-start.2) | async-done | bytes 2097184 | tf_op jit(solution)/shard_map/all_to_all | solution.py:188
  213.3 3.7 fusion.90
  217.0 10.0 %fusion.22 = (f32[2,64,4,16]{1,3,2,0:T(8,128)}, f32[2,64,4,16]{1,3,2,0:T(8,128)S(1)}, f32[2,4,16,64,64]{4,3,2,1,0:T(8,128)}) fusion(f32[2,64,4,16,64]{1,4,3,2,0:T(8,128)S(1)} %copy-done, f32[4,16,64,2,64]{4,2,1,0,3:T(8,128)S(1)} %fusion.90, f32[2,4,16,64,128]{4,3,2,1,0:T(8,128)} %get-tuple-element.578, f32[2,64,4,128,1]{3,2,1,0,4:T(4,128)S(1)} %bitcast.257), kind=kOutput, calls=%fused_computation.45 | convolution fusion | flops 807387136 | bytes 10813440 | tf_op jit(solution)/shard_map/jvp(ctgn,cgrpn->ctgrp)/dot_general | solution.py:97
  227.7 3.6 fusion.23
  235.7 4.1 copy.317
  239.8 6.6 %all-to-all-start.3 = ((f32[64,16,512]{2,0,1:T(8,128)}), f32[64,16,512]{2,0,1:T(8,128)}, u32[]{:S(2)}, u32[]{:S(2)}) async-start(f32[64,16,512]{2,0,1:T(8,128)} %copy.317), calls=%async_computation.3 | async-start | bytes 4194304 | tf_op jit(solution)/shard_map/all_to_all | solution.py:202
  246.5 45.7 %all-to-all-done.3 = f32[64,16,512]{2,0,1:T(8,128)} async-done(((f32[64,16,512]{2,0,1:T(8,128)}), f32[64,16,512]{2,0,1:T(8,128)}, u32[]{:S(2)}, u32[]{:S(2)}) %all-to-all-start.3) | async-done | bytes 2097184 | tf_op jit(solution)/shard_map/all_to_all | solution.py:202
  304.4 4.1 pad.105
  318.2 6.4 %pad.145 = f32[64,15,512]{2,0,1:T(8,128)} pad(f32[64,8,512]{2,0,1:T(8,128)} %pad_maximum_fusion.2, f32[]{:T(128)} %constant.116.clone.1), padding=0_0_0x0_0_1x0_0_0 | pad | bytes 3014660 | tf_op jit(solution)/shard_map/slice | solution.py:121
  324.6 6.5 %pad.222 = f32[64,16,512]{2,0,1:T(8,128)} pad(f32[64,8,512]{2,0,1:T(8,128)} %add.278, f32[]{:T(128)} %constant.116.clone.1), padding=0_0_0x1_0_1x0_0_0 | pad | bytes 3145732
  331.1 3.9 slice_add_fusion.7
  341.2 6.6 %all-to-all-start.4 = ((f32[64,16,512]{2,0,1:T(8,128)}), f32[64,16,512]{2,0,1:T(8,128)}, u32[]{:S(2)}, u32[]{:S(2)}) async-start(f32[64,16,512]{2,0,1:T(8,128)} %concatenate.42), calls=%async_computation.4 | async-start | bytes 4194304 | tf_op jit(solution)/shard_map/all_to_all | solution.py:207
  347.8 4.5 reshape.292
  352.5 4.9 copy.307
  358.8 9.6 %fusion.43 = (f32[2,4,16,64]{3,2,1,0:T(8,128)}, f32[2,4,16,64]{3,2,1,0:T(8,128)}, f32[2,4,16,64]{3,2,1,0:T(8,128)}, f32[2,4,64,64]{3,2,1,0:T(8,128)}) fusion(f32[2,4,16,64]{3,2,1,0:T(8,128)S(1)} %copy.291, f32[2,4,16,64]{3,2,1,0:T(8,128)S(1)} %copy.289, f32[2,4,64,64]{3,2,1,0:T(8,128)S(1)} %fusion.85, pred[2,64,64]{2,1,0:T(8,128)(4,1)S(1)} %compare_and_fusion, ...), kind=kOutput, calls=%fused_computation.79 | convolution fusion | flops 409411584 | bytes 3579904 | tf_op jit(solution)/shard_map/transpose(jvp(cgrts,csgrp->ctgrp))/dot_general | solution.py:95
  368.5 9.6 %fusion.18 = bf16[2,64,4,16,64]{1,4,3,2,0:T(8,128)(2,1)} fusion(f32[4,16,64,2,64]{4,2,1,0,3:T(8,128)S(1)} %copy-done.14, f32[2,4,16,64,64]{4,3,2,1,0:T(8,128)S(1)} %copy-done.17, f32[2,64,4,16,64]{1,4,3,2,0:T(8,128)S(1)} %copy-done.6, f32[2,64,4,16]{1,3,2,0:T(8,128)S(1)} %copy-done.39, f32[4,16]{1,0:T(4,128)S(1)} %mul.662, ...), kind=kOutput, calls=%fused_computation.39 | convolution fusion | flops 408420352 | bytes 7610624 | tf_op jit(solution)/shard_map/jvp(cgrts,csgrp->ctgrp)/dot_general | solution.py:95
  378.1 5.3 copy.304
  383.4 4.5 convert_element_type.79
  387.9 9.1 %convolution_bitcast_fusion.1 = f32[2,64,4,128]{3,1,2,0:T(8,128)S(1)} fusion(f32[4,16,64,128,1]{3,2,1,0,4:T(8,128)S(1)} %reshape.310, f32[2,64,4,16,64]{1,4,3,2,0:T(8,128)} %copy.305, f32[2,64,4,16]{1,3,2,0:T(8,128)S(1)} %copy-done.39), kind=kOutput, calls=%fused_computation.108 | convolution fusion | flops 805830656 | bytes 4489216 | tf_op jit(solution)/shard_map/transpose(jvp(ctgn,grpn->ctgrp))/dot_general | solution.py:105
  397.1 8.9 %fusion.70 = f32[2,4,64,128]{3,2,1,0:T(8,128)S(1)} fusion(f32[2,4,16,64,128]{4,3,2,1,0:T(8,128)} %get-tuple-element.578, f32[2,64,4,16,64]{1,4,3,2,0:T(8,128)S(1)} %copy-done.1, f32[2,64,4,16]{1,3,2,0:T(8,128)S(1)} %get-tuple-element.358), kind=kOutput, calls=%fused_computation.105 | convolution fusion | flops 805830656 | bytes 6586368 | tf_op jit(solution)/shard_map/transpose(jvp(ctgn,cgrpn->ctgrp))/dot_general | solution.py:97
  407.3 5.5 fusion.13
  414.9 4.1 copy.318
  423.1 10.6 %while.39 = (s32[]{:T(128)}, f32[4,16]{1,0:T(4,128)S(1)}, f32[4,16,64,128]{3,2,1,0:T(8,128)S(1)}, f32[2,4,16]{2,1,0:T(4,128)S(1)}, f32[2,4,16,64,128]{4,3,2,1,0:...) while((s32[]{:T(128)}, f32[4,16]{1,0:T(4,128)S(1)}, ...), condition=%wide.region_12.13_spmd, body=%wide.region_10.12_spmd.sunk | while | flops 2097347 | bytes 29370552 | solution.py:78
  433.8 7.9 %fusion.11 = (f32[2,64,4,16]{1,3,2,0:T(8,128)}, f32[2,4,16,64,64]{4,3,2,1,0:T(8,128)S(1)}) fusion(f32[2,64,4,16,64]{1,4,3,2,0:T(8,128)} %copy.292, f32[2,4,16,64,128]{4,3,2,1,0:T(8,128)} %get-tuple-element.274, f32[2,64,4,128,1]{3,2,1,0,4:T(4,128)S(1)} %bitcast.263), kind=kOutput, calls=%fused_computation.27 | convolution fusion | flops 806346752 | bytes 8683520 | tf_op jit(solution)/shard_map/transpose(jvp(cqgrp,cqgn->cgrpn))/dot_general | solution.py:68
  441.7 7.9 %fusion.67 = f32[2,64,4,128]{3,1,2,0:T(8,128)} fusion(f32[2,4,16,64,128]{4,3,2,1,0:T(8,128)S(1)} %copy-done.12, f32[2,64,4,16,64]{1,4,3,2,0:T(8,128)S(1)} %copy-done.7, f32[2,64,4,16]{1,3,2,0:T(8,128)S(1)} %copy-done.37), kind=kOutput, calls=%fused_computation.104 | convolution fusion | flops 805830656 | bytes 6586368 | tf_op jit(solution)/shard_map/transpose(jvp(cqgrp,cqgn->cgrpn))/dot_general | solution.py:68
  449.7 5.8 fusion.10
  455.4 6.3 %copy.327 = f32[2,64,4,16,64]{4,3,2,1,0:T(8,128)} copy(f32[2,64,4,16,64]{1,4,3,2,0:T(8,128)} %fusion.10) | data formatting | bytes 4194304 | tf_op jit(solution)/shard_map/add | solution.py:216
  461.7 4.9 reshape.297
  469.6 5.0 multiply_reduce_fusion.4
  481.4 3.2 collective-permute-start.1
  491.8 24.6 %psum.15 = f32[3,64]{1,0:T(4,128)S(1)} all-reduce(f32[3,64]{1,0:T(4,128)S(1)} %pad_maximum_fusion.8), channel_id=1, replica_groups=mesh['groups'=2,'ctx'=16] {'ctx'}, use_global_device_ids=true, to_apply=%region_30.31 | all-reduce | flops 192 | bytes 1536 | tf_op jit(solution)/shard_map/psum | solution.py:230
  519.8 59.7 %all-reduce.33.cloned.1.call-done = f32[5,5120]{1,0:T(8,128)} async-done(((f32[5,5120]{1,0:T(8,128)}), f32[5,5120]{1,0:T(8,128)}) %all-reduce.33.cloned.1.call-update) | async-done | bytes 102416 | tf_op jit(solution)/shard_map/psum | solution.py:230
  (351 shorter events, 132.6 us)
Async XLA Ops:
  7.2 11.1 %copy-start.35 = (bf16[128,5120]{1,0:T(8,128)(2,1)S(1)}, bf16[128,5120]{1,0:T(8,128)(2,1)}, u32[]{:S(2)}) copy-start(bf16[128,5120]{1,0:T(8,128)(2,1)} %param.13) | copy-start | bytes 3932164
  8.8 9.5 %collective-permute-start = (bf16[3,5120]{1,0:T(4,128)(2,1)}, bf16[3,5120]{1,0:T(4,128)(2,1)}, u32[]{:S(2)}, u32[]{:S(2)}) collective-permute-start(bf16[3,5120]{1,0:T(4,128)(2,1)} %slice.256), channel_id=1, source_target_pairs={{0,1},{1,2},{2,3},{3,4},{4,5},{5,6},{6,7},{7,8},{8,9},{9,10},{10,1... | collective-permute-start | bytes 92168 | tf_op jit(solution)/shard_map/ppermute | solution.py:15
  12.4 7.1 %copy-start.71 = (f32[128]{0:T(128)}, f32[128]{0:T(128)S(1)}, u32[]{:S(2)}) copy-start(f32[128]{0:T(128)S(1)} %get-tuple-element.361) | copy-start | bytes 1540
  17.3 5.4 copy-start.49
  17.3 5.4 copy-start.51
  17.5 19.7 %copy-start.36 = (f32[2,64,4,16]{1,3,2,0:T(8,128)}, f32[2,64,4,16]{1,3,2,0:T(8,128)S(1)}, u32[]{:S(2)}) copy-start(f32[2,64,4,16]{1,3,2,0:T(8,128)S(1)} %copy_multiply_fusion) | copy-start | bytes 98308
  53.4 13.0 %copy-start.60 = (f32[2,4,16,1,1]{2,1,4,3,0:T(4,128)}, f32[2,4,16,1,1]{2,1,4,3,0:T(4,128)S(1)}, u32[]{:S(2)}) copy-start(f32[2,4,16,1,1]{2,1,4,3,0:T(4,128)S(1)} %get-tuple-element.577) | copy-start | bytes 1540
  54.1 12.3 %all-to-all-start.1 = ((f32[64,16,1]{0,2,1:T(1,128)}), f32[64,16,1]{0,2,1:T(1,128)S(1)}, u32[]{:S(2)}, u32[]{:S(2)}) async-start(f32[64,16,1]{0,2,1:T(1,128)} %broadcast_in_dim.115), calls=%async_computation.1 | async-start | bytes 16384 | tf_op jit(solution)/shard_map/all_to_all | solution.py:184
  66.4 52.3 %all-to-all-start = ((f32[64,16,512]{2,0,1:T(8,128)}), f32[64,16,512]{2,0,1:T(8,128)S(1)}, u32[]{:S(2)}, u32[]{:S(2)}) async-start(f32[64,16,512]{2,0,1:T(8,128)} %copy.300), calls=%async_computation | async-start | bytes 4194304 | tf_op jit(solution)/shard_map/all_to_all | solution.py:183
  120.2 8.5 %copy-start.79 = (f32[64,3,1]{0,1,2:T(4,128)S(1)}, f32[64,3,1]{0,1,2:T(4,128)}, u32[]{:S(2)}) copy-start(f32[64,3,1]{0,1,2:T(4,128)} %copy.423) | copy-start | bytes 2308
  124.2 10.7 %slice-start.1 = ((f32[64,8,512]{2,0,1:T(8,128)}), f32[64,1,512]{2,0,1:T(8,128)S(1)}, s32[]{:S(2)}) async-start(f32[64,8,512]{2,0,1:T(8,128)} %copy-done.26), calls=%async_computation.7 | async-start | bytes 262144 | tf_op jit(solution)/shard_map/slice | solution.py:118
  136.7 7.0 %copy-start.67 = (f32[64,7,1]{0,1,2:T(8,128)S(1)}, f32[64,7,1]{0,1,2:T(8,128)}, u32[]{:S(2)}) copy-start(f32[64,7,1]{0,1,2:T(8,128)} %copy.421) | copy-start | bytes 5380
  155.5 52.3 %all-to-all-start.2 = ((f32[64,16,512]{2,0,1:T(8,128)}), f32[64,16,512]{2,0,1:T(8,128)S(1)}, u32[]{:S(2)}, u32[]{:S(2)}) async-start(f32[64,16,512]{2,0,1:T(8,128)} %concatenate.38), calls=%async_computation.2 | async-start | bytes 4194304 | tf_op jit(solution)/shard_map/all_to_all | solution.py:188
  165.2 5.9 %copy-start.42 = (f32[128,512]{1,0:T(8,128)S(1)}, f32[128,512]{1,0:T(8,128)}, u32[]{:S(2)}) copy-start(f32[128,512]{1,0:T(8,128)} %get-tuple-element.371) | copy-start | bytes 786436
  217.0 10.0 %copy-start.13 = (f32[4,16,64,2,64]{4,2,1,0,3:T(8,128)}, f32[4,16,64,2,64]{4,2,1,0,3:T(8,128)S(1)}, u32[]{:S(2)}) copy-start(f32[4,16,64,2,64]{4,2,1,0,3:T(8,128)S(1)} %fusion.90) | copy-start | bytes 6291460
  217.0 10.0 %copy-start.31 = (f32[2,64,4,16]{1,3,2,0:T(8,128)S(1)}, f32[2,64,4,16]{1,3,2,0:T(8,128)}, u32[]{:S(2)}) copy-start(f32[2,64,4,16]{1,3,2,0:T(8,128)} %copy-done.30) | copy-start | bytes 98308
  217.0 10.0 %copy-start.69 = (f32[2,64]{1,0:T(2,128)S(1)}, f32[2,64]{1,0:T(2,128)}, u32[]{:S(2)}) copy-start(f32[2,64]{1,0:T(2,128)} %get-tuple-element.405) | copy-start | bytes 1540
  239.8 6.6 %copy-start.59 = (f32[64,8,1]{0,2,1:T(1,128)S(1)}, f32[64,8,1]{0,2,1:T(1,128)}, u32[]{:S(2)}) copy-start(f32[64,8,1]{0,2,1:T(1,128)} %get-tuple-element.394) | copy-start | bytes 6148
  239.8 6.6 %copy-start.68 = (f32[64,7,1]{0,2,1:T(1,128)S(1)}, f32[64,7,1]{0,2,1:T(1,128)}, u32[]{:S(2)}) copy-start(f32[64,7,1]{0,2,1:T(1,128)} %get-tuple-element.392) | copy-start | bytes 5380
  239.8 52.5 %all-to-all-start.3 = ((f32[64,16,512]{2,0,1:T(8,128)}), f32[64,16,512]{2,0,1:T(8,128)}, u32[]{:S(2)}, u32[]{:S(2)}) async-start(f32[64,16,512]{2,0,1:T(8,128)} %copy.317), calls=%async_computation.3 | async-start | bytes 4194304 | tf_op jit(solution)/shard_map/all_to_all | solution.py:202
  298.0 10.5 %slice-start = ((f32[64,8,512]{2,0,1:T(8,128)}), f32[64,1,512]{2,0,1:T(8,128)S(1)}, s32[]{:S(2)}) async-start(f32[64,8,512]{2,0,1:T(8,128)} %copy-done.25), calls=%async_computation.6 | async-start | bytes 262144 | tf_op jit(solution)/shard_map/slice | solution.py:118
  341.2 71.7 %all-to-all-start.4 = ((f32[64,16,512]{2,0,1:T(8,128)}), f32[64,16,512]{2,0,1:T(8,128)}, u32[]{:S(2)}, u32[]{:S(2)}) async-start(f32[64,16,512]{2,0,1:T(8,128)} %concatenate.42), calls=%async_computation.4 | async-start | bytes 4194304 | tf_op jit(solution)/shard_map/all_to_all | solution.py:207
  347.8 231.6 %all-reduce.33.cloned.1.call-start = ((), (), s32[]{:S(2)}) async-start(), calls=%async_computation.5 | async-start | bytes 327680 | tf_op jit(solution)/shard_map/psum | solution.py:230
  358.8 9.7 %copy-start.6 = (f32[2,64,4,16,64]{1,4,3,2,0:T(8,128)S(1)}, f32[2,64,4,16,64]{1,4,3,2,0:T(8,128)}, u32[]{:S(2)}) copy-start(f32[2,64,4,16,64]{1,4,3,2,0:T(8,128)} %copy.292) | copy-start | bytes 6291460
  358.8 9.7 %copy-start.14 = (f32[4,16,64,2,64]{4,2,1,0,3:T(8,128)S(1)}, f32[4,16,64,2,64]{4,2,1,0,3:T(8,128)}, u32[]{:S(2)}) copy-start(f32[4,16,64,2,64]{4,2,1,0,3:T(8,128)} %copy-done.13) | copy-start | bytes 6291460
  358.8 9.7 %copy-start.17 = (f32[2,4,16,64,64]{4,3,2,1,0:T(8,128)S(1)}, f32[2,4,16,64,64]{4,3,2,1,0:T(8,128)}, u32[]{:S(2)}) copy-start(f32[2,4,16,64,64]{4,3,2,1,0:T(8,128)} %get-tuple-element.410) | copy-start | bytes 6291460
  358.8 9.7 %copy-start.39 = (f32[2,64,4,16]{1,3,2,0:T(8,128)S(1)}, f32[2,64,4,16]{1,3,2,0:T(8,128)}, u32[]{:S(2)}) copy-start(f32[2,64,4,16]{1,3,2,0:T(8,128)} %copy-done.38) | copy-start | bytes 98308
  387.9 9.2 %copy-start.1 = (f32[2,64,4,16,64]{1,4,3,2,0:T(8,128)S(1)}, f32[2,64,4,16,64]{1,4,3,2,0:T(8,128)}, u32[]{:S(2)}) copy-start(f32[2,64,4,16,64]{1,4,3,2,0:T(8,128)} %copy.305) | copy-start | bytes 6291460
  397.1 8.9 %copy-start.40 = (f32[2,4,64,64]{3,2,1,0:T(8,128)S(1)}, f32[2,4,64,64]{3,2,1,0:T(8,128)}, u32[]{:S(2)}) copy-start(f32[2,4,64,64]{3,2,1,0:T(8,128)} %get-tuple-element.310) | copy-start | bytes 393220
  407.3 5.6 copy-start.16
  433.8 8.0 %copy-start.7 = (f32[2,64,4,16,64]{1,4,3,2,0:T(8,128)S(1)}, f32[2,64,4,16,64]{1,4,3,2,0:T(8,128)}, u32[]{:S(2)}) copy-start(f32[2,64,4,16,64]{1,4,3,2,0:T(8,128)} %copy.292) | copy-start | bytes 6291460
  433.8 7.9 %copy-start.12 = (f32[2,4,16,64,128]{4,3,2,1,0:T(8,128)S(1)}, f32[2,4,16,64,128]{4,3,2,1,0:T(8,128)}, u32[]{:S(2)}) copy-start(f32[2,4,16,64,128]{4,3,2,1,0:T(8,128)} %get-tuple-element.274) | copy-start | bytes 12582916
  433.8 7.9 %copy-start.37 = (f32[2,64,4,16]{1,3,2,0:T(8,128)S(1)}, f32[2,64,4,16]{1,3,2,0:T(8,128)}, u32[]{:S(2)}) copy-start(f32[2,64,4,16]{1,3,2,0:T(8,128)} %copy-done.36) | copy-start | bytes 98308
  441.7 7.9 %copy-start.2 = (f32[2,64,4,16,64]{1,4,3,2,0:T(8,128)S(1)}, f32[2,64,4,16,64]{1,4,3,2,0:T(8,128)}, u32[]{:S(2)}) copy-start(f32[2,64,4,16,64]{1,4,3,2,0:T(8,128)} %copy.305) | copy-start | bytes 6291460
  441.7 7.9 %copy-start.24 = (bf16[2,64,4,16,64]{1,4,3,2,0:T(8,128)(2,1)S(1)}, bf16[2,64,4,16,64]{1,4,3,2,0:T(8,128)(2,1)}, u32[]{:S(2)}) copy-start(bf16[2,64,4,16,64]{1,4,3,2,0:T(8,128)(2,1)} %copy.307) | copy-start | bytes 3145732
  461.7 7.8 %copy-start.4 = (f32[131,5120]{1,0:T(8,128)S(1)}, f32[131,5120]{1,0:T(8,128)}, u32[]{:S(2)}) copy-start(f32[131,5120]{1,0:T(8,128)} %copy-done.3) | copy-start | bytes 8048644
  479.1 5.6 copy-start.84
  479.1 6.5 %copy-start.34 = (f32[2,64,4,16]{1,0,3,2:T(2,128)S(1)}, f32[2,64,4,16]{1,0,3,2:T(2,128)}, u32[]{:S(2)}) copy-start(f32[2,64,4,16]{1,0,3,2:T(2,128)} %copy-done.32) | copy-start | bytes 98308
  479.1 6.5 %copy-start.45 = (f32[2,64,4,16]{1,3,2,0:T(8,128)S(1)}, f32[2,64,4,16]{1,3,2,0:T(8,128)}, u32[]{:S(2)}) copy-start(f32[2,64,4,16]{1,3,2,0:T(8,128)} %get-tuple-element.411) | copy-start | bytes 98308
  479.1 6.5 %copy-start.58 = (f32[2,4,16]{2,1,0:T(4,128)S(1)}, f32[2,4,16]{2,1,0:T(4,128)}, u32[]{:S(2)}) copy-start(f32[2,4,16]{2,1,0:T(4,128)} %copy-done.57) | copy-start | bytes 1540
  479.1 6.5 %copy-start.64 = (f32[2,64]{1,0:T(2,128)S(1)}, f32[2,64]{1,0:T(2,128)}, u32[]{:S(2)}) copy-start(f32[2,64]{1,0:T(2,128)} %copy-done.63) | copy-start | bytes 1540
  479.1 6.8 %copy-start.44 = (f32[2,64,4,16]{1,3,2,0:T(8,128)S(1)}, f32[2,64,4,16]{1,3,2,0:T(8,128)}, u32[]{:S(2)}) copy-start(f32[2,64,4,16]{1,3,2,0:T(8,128)} %copy-done.43) | copy-start | bytes 98308
  479.1 6.8 %copy-start.46 = (f32[2,64,4,16]{1,3,2,0:T(8,128)S(1)}, f32[2,64,4,16]{1,3,2,0:T(8,128)}, u32[]{:S(2)}) copy-start(f32[2,64,4,16]{1,3,2,0:T(8,128)} %get-tuple-element.311) | copy-start | bytes 98308
  479.1 6.8 %copy-start.70 = (f32[2,64]{1,0:T(2,128)S(1)}, f32[2,64]{1,0:T(2,128)}, u32[]{:S(2)}) copy-start(f32[2,64]{1,0:T(2,128)} %get-tuple-element.405) | copy-start | bytes 1540
  481.4 8.2 %copy-start.55 = (f32[128,64]{0,1:T(8,128)S(1)}, f32[128,64]{0,1:T(8,128)}, u32[]{:S(2)}) copy-start(f32[128,64]{0,1:T(8,128)} %param.14) | copy-start | bytes 98308
  481.4 8.2 %copy-start.80 = (f32[64]{0:T(128)S(1)}, f32[64]{0:T(128)}, u32[]{:S(2)}) copy-start(f32[64]{0:T(128)} %param.15) | copy-start | bytes 772
  481.4 8.2 %copy-start.82 = (f32[64]{0:T(128)S(1)}, f32[64]{0:T(128)}, u32[]{:S(2)}) copy-start(f32[64]{0:T(128)} %copy-done.81) | copy-start | bytes 772
  481.4 99.6 %collective-permute-start.1 = (f32[3,5120]{1,0:T(4,128)S(1)}, f32[3,5120]{1,0:T(4,128)S(1)}, u32[]{:S(2)}, u32[]{:S(2)}) collective-permute-start(f32[3,5120]{1,0:T(4,128)S(1)} %pad_add_fusion.3), channel_id=1, source_target_pairs={{1,0},{2,1},{3,2},{4,3},{5,4},{6,5},{7,6},{8,7},{9,8},{10,9},{11,1... | collective-permute-start | bytes 184328 | tf_op jit(solution)/shard_map/ppermute | solution.py:15
  (50 other events, 155.4 us)
Sparse Core Ops, SparseCore 0:
  489.7 89.6 all-reduce.32
where the time goes:
time: 601 us; the launch traced here: 591 us
  waiting for transfers between devices  185 us (31%)
  local copies, waits for them, and re-layouts  166 us (28%)
  matrix products  91.3 us (15%)
  other arithmetic  69.4 us (12%)
  starting transfers between devices  37.9 us (6%)
  blocking collectives  24.6 us (4%)
  between operations  15.6 us (3%)
    psum x1, waiting for transfers between devices, body(): lax.psum((jnp.concatenate([grad_kernel, grad_kernel_bias[None, :]], axis=...  59.7 us
    all_to_all x1, waiting for transfers between devices, body(): lax.all_to_all(flat_grads, 'ctx', split_axis=1, concat_axis=1, tiled=True)  45.7 us
    all_to_all x1, waiting for transfers between devices, body(): lax.all_to_all(flat_states, 'ctx', split_axis=1, concat_axis=1, tiled=True)  43.4 us
    all_to_all x2, waiting for transfers between devices, body(): lax.all_to_all(ready, 'ctx', split_axis=1, concat_axis=1, tiled=True)  36.5 us
    dot_general x3, matrix products, out_part(): y_diag = jnp.einsum('cgrts,csgrp->ctgrp', weights, inputs, precision=HIGH)  25 us
    psum x1, blocking collectives, body(): lax.psum((jnp.concatenate([grad_kernel, grad_kernel_bias[None, :]], axis=...  24.6 us
    dot_general x3, matrix products, out_part(): jnp.einsum('ctgn,cgrpn->ctgrp', c_values, b_chain, precision=HIGH)  24.4 us
    pad x8, local copies, waits for them, and re-layouts, owner_prefix(): lax.associative_scan(owner_join, (factors, values), reverse=reverse, axis=1)  22.9 us
  transfers between devices with their start and end apart: 8, of which 4 were waited for; matrix products, arithmetic and copies ran while one was open for 17% of the time, Pallas kernels for 0%

commit v1 on v0

--- a/solution.py
+++ b/solution.py
@@ -180,7 +180,12 @@
     flat_states = state_all.reshape(heads, devices, -1)
     ready = owner_prefix(
         (
-            lax.all_to_all(flat_states, "ctx", split_axis=1, concat_axis=1, tiled=True),
+            jnp.concatenate(
+                lax.all_to_all(
+                    jnp.stack(jnp.split(flat_states, lax.axis_size("ctx"), axis=1)), "ctx", 0, 0
+                ),
+                axis=1,
+            ),
             lax.all_to_all(rates, "ctx", split_axis=1, concat_axis=1, tiled=True),
         ),
         False,

time: 601 us -> 623 us (1.037)
  local copies, waits for them, and re-layouts: 166 us -> 187 us
    unnamed x174 -> x191, local copies, waits for them, and re-layouts: 19 us -> 39.9 us
  transfers between devices with their start and end apart: 8 -> 8, of which waited for: 4 -> 5; matrix products, arithmetic and copies ran while one was open for 17% -> 16% of each run, Pallas kernels for 0% -> 0%
where the time goes in v1:
time: 623 us; the launch traced here: 612 us
  local copies, waits for them, and re-layouts  187 us (30%)
  waiting for transfers between devices  187 us (30%)
  matrix products  91.3 us (15%)
  other arithmetic  69.5 us (11%)
  starting transfers between devices  36.9 us (6%)
  blocking collectives  24.6 us (4%)
  between operations  15.7 us (3%)
    psum x1, waiting for transfers between devices, body(): lax.psum((jnp.concatenate([grad_kernel, grad_kernel_bias[None, :]], axis=...  59.6 us
    all_to_all x1, waiting for transfers between devices, body(): lax.all_to_all(flat_grads, 'ctx', split_axis=1, concat_axis=1, tiled=True)  45.7 us
    all_to_all x1, waiting for transfers between devices, body(): lax.all_to_all(jnp.stack(jnp.split(flat_states, lax.axis_size('ctx'), axi...  43.4 us
    unnamed x191, local copies, waits for them, and re-layouts  39.9 us
    all_to_all x2, waiting for transfers between devices, body(): lax.all_to_all(ready, 'ctx', split_axis=1, concat_axis=1, tiled=True)  36.5 us
    dot_general x3, matrix products, out_part(): y_diag = jnp.einsum('cgrts,csgrp->ctgrp', weights, inputs, precision=HIGH)  25 us
    psum x1, blocking collectives, body(): lax.psum((jnp.concatenate([grad_kernel, grad_kernel_bias[None, :]], axis=...  24.6 us
    dot_general x3, matrix products, out_part(): jnp.einsum('ctgn,cgrpn->ctgrp', c_values, b_chain, precision=HIGH)  24.5 us
  transfers between devices with their start and end apart: 8, of which 5 were waited for; matrix products, arithmetic and copies ran while one was open for 16% of the time, Pallas kernels for 0%

profile of v1, /device:TPU:8, one launch (start us, length us, event | category | flops | bytes accessed | tf_op | source)
XLA Modules:
  0.0 612.1 jit_solution(13967640954085595676)
XLA Ops:
  19.5 3.2 fusion.41
  25.7 4.7 reshape.290
  30.4 5.8 copy.322
  37.3 7.0 %fusion.35 = f32[2,4,16,64,128]{4,3,2,1,0:T(8,128)} fusion(f32[2,64,4,16,64]{1,4,3,2,0:T(8,128)} %copy.322, f32[2,64,4,16]{1,3,2,0:T(8,128)S(1)} %copy_multiply_fusion, f32[2,64,4,128,1]{3,2,1,0,4:T(4,128)S(1)} %bitcast.332), kind=kOutput, calls=%fused_computation.60 | convolution fusion | flops 805830656 | bytes 6586368 | tf_op jit(solution)/shard_map/jvp(cqgrp,cqgn->cgrpn)/dot_general | solution.py:68
  46.8 6.6 %while.40 = (s32[]{:T(128)}, f32[4,16]{1,0:T(4,128)S(1)}, f32[4,16,64,128]{3,2,1,0:T(8,128)S(1)}, f32[2,4,16]{2,1,0:T(4,128)S(1)}, f32[2,4,16,64,128]{4,3,2,1,0:...) while((s32[]{:T(128)}, f32[4,16]{1,0:T(4,128)S(1)}, ...), condition=%wide.region_5.6_spmd.clone, body=%wide.region_4.5_spmd.clone.sunk | while | flops 2097347 | bytes 27272616 | solution.py:78
  76.0 6.6 %all-to-all-start.1 = ((f32[64,16,1]{0,2,1:T(1,128)}), f32[64,16,1]{0,2,1:T(1,128)S(1)}, u32[]{:S(2)}, u32[]{:S(2)}) async-start(f32[64,16,1]{0,2,1:T(1,128)} %broadcast_in_dim.115), calls=%async_computation.1 | async-start | bytes 16384 | tf_op jit(solution)/shard_map/all_to_all | solution.py:189
  87.4 5.6 all-to-all-start
  95.4 43.4 %all-to-all-done = f32[16,64,1,512]{3,1,2,0:T(8,128)S(1)} async-done(((f32[16,64,1,512]{3,1,2,0:T(8,128)}), f32[16,64,1,512]{3,1,2,0:T(8,128)S(1)}, u32[]{:S(2)}, u32[]{:S(2)}) %all-to-all-start) | async-done | bytes 2097184 | tf_op jit(solution)/shard_map/all_to_all | solution.py:184
  151.5 4.1 pad.96
  157.4 4.1 pad.95
  165.4 4.1 pad.143
  169.5 3.9 pad.221
  176.9 6.4 %all-to-all-start.2 = ((f32[64,16,512]{2,0,1:T(8,128)}), f32[64,16,512]{2,0,1:T(8,128)S(1)}, u32[]{:S(2)}, u32[]{:S(2)}) async-start(f32[64,16,512]{2,0,1:T(8,128)} %concatenate.38), calls=%async_computation.2 | async-start | bytes 4194304 | tf_op jit(solution)/shard_map/all_to_all | solution.py:193
  183.3 3.3 reshape.299
  186.6 5.9 copy.335
  192.7 36.5 %all-to-all-done.2 = f32[64,16,512]{2,0,1:T(8,128)S(1)} async-done(((f32[64,16,512]{2,0,1:T(8,128)}), f32[64,16,512]{2,0,1:T(8,128)S(1)}, u32[]{:S(2)}, u32[]{:S(2)}) %all-to-all-start.2) | async-done | bytes 2097184 | tf_op jit(solution)/shard_map/all_to_all | solution.py:193
  234.7 3.7 fusion.90
  238.4 10.0 %fusion.22 = (f32[2,64,4,16]{1,3,2,0:T(8,128)}, f32[2,64,4,16]{1,3,2,0:T(8,128)S(1)}, f32[2,4,16,64,64]{4,3,2,1,0:T(8,128)}) fusion(f32[2,64,4,16,64]{1,4,3,2,0:T(8,128)S(1)} %copy-done, f32[4,16,64,2,64]{4,2,1,0,3:T(8,128)S(1)} %fusion.90, f32[2,4,16,64,128]{4,3,2,1,0:T(8,128)} %get-tuple-element.578, f32[2,64,4,128,1]{3,2,1,0,4:T(4,128)S(1)} %bitcast.327), kind=kOutput, calls=%fused_computation.45 | convolution fusion | flops 807387136 | bytes 10813440 | tf_op jit(solution)/shard_map/jvp(ctgn,cgrpn->ctgrp)/dot_general | solution.py:97
  249.1 3.6 fusion.23
  257.1 4.1 copy.347
  261.2 6.6 %all-to-all-start.3 = ((f32[64,16,512]{2,0,1:T(8,128)}), f32[64,16,512]{2,0,1:T(8,128)}, u32[]{:S(2)}, u32[]{:S(2)}) async-start(f32[64,16,512]{2,0,1:T(8,128)} %copy.347), calls=%async_computation.3 | async-start | bytes 4194304 | tf_op jit(solution)/shard_map/all_to_all | solution.py:207
  267.9 45.7 %all-to-all-done.3 = f32[64,16,512]{2,0,1:T(8,128)} async-done(((f32[64,16,512]{2,0,1:T(8,128)}), f32[64,16,512]{2,0,1:T(8,128)}, u32[]{:S(2)}, u32[]{:S(2)}) %all-to-all-start.3) | async-done | bytes 2097184 | tf_op jit(solution)/shard_map/all_to_all | solution.py:207
  325.8 4.1 pad.105
  339.6 6.4 %pad.145 = f32[64,15,512]{2,0,1:T(8,128)} pad(f32[64,8,512]{2,0,1:T(8,128)} %pad_maximum_fusion.2, f32[]{:T(128)} %constant.116.clone.1), padding=0_0_0x0_0_1x0_0_0 | pad | bytes 3014660 | tf_op jit(solution)/shard_map/slice | solution.py:121
  346.0 6.5 %pad.222 = f32[64,16,512]{2,0,1:T(8,128)} pad(f32[64,8,512]{2,0,1:T(8,128)} %add.278, f32[]{:T(128)} %constant.116.clone.1), padding=0_0_0x1_0_1x0_0_0 | pad | bytes 3145732
  352.5 3.9 slice_add_fusion.7
  359.5 3.1 concatenate.42
  362.6 6.6 %all-to-all-start.4 = ((f32[64,16,512]{2,0,1:T(8,128)}), f32[64,16,512]{2,0,1:T(8,128)}, u32[]{:S(2)}, u32[]{:S(2)}) async-start(f32[64,16,512]{2,0,1:T(8,128)} %concatenate.42), calls=%async_computation.4 | async-start | bytes 4194304 | tf_op jit(solution)/shard_map/all_to_all | solution.py:212
  369.2 4.5 reshape.300
  373.9 4.9 copy.337
  380.2 9.7 %fusion.43 = (f32[2,4,16,64]{3,2,1,0:T(8,128)}, f32[2,4,16,64]{3,2,1,0:T(8,128)}, f32[2,4,16,64]{3,2,1,0:T(8,128)}, f32[2,4,64,64]{3,2,1,0:T(8,128)}) fusion(f32[2,4,16,64]{3,2,1,0:T(8,128)S(1)} %copy.321, f32[2,4,16,64]{3,2,1,0:T(8,128)S(1)} %copy.319, f32[2,4,64,64]{3,2,1,0:T(8,128)S(1)} %fusion.85, pred[2,64,64]{2,1,0:T(8,128)(4,1)S(1)} %compare_and_fusion, ...), kind=kOutput, calls=%fused_computation.79 | convolution fusion | flops 409411584 | bytes 3579904 | tf_op jit(solution)/shard_map/transpose(jvp(cgrts,csgrp->ctgrp))/dot_general | solution.py:95
  389.9 9.6 %fusion.18 = bf16[2,64,4,16,64]{1,4,3,2,0:T(8,128)(2,1)} fusion(f32[4,16,64,2,64]{4,2,1,0,3:T(8,128)S(1)} %copy-done.14, f32[2,4,16,64,64]{4,3,2,1,0:T(8,128)S(1)} %copy-done.17, f32[2,64,4,16,64]{1,4,3,2,0:T(8,128)S(1)} %copy-done.6, f32[2,64,4,16]{1,3,2,0:T(8,128)S(1)} %copy-done.39, f32[4,16]{1,0:T(4,128)S(1)} %mul.662, ...), kind=kOutput, calls=%fused_computation.39 | convolution fusion | flops 408420352 | bytes 7610624 | tf_op jit(solution)/shard_map/jvp(cgrts,csgrp->ctgrp)/dot_general | solution.py:95
  399.5 5.3 copy.334
  404.8 4.5 convert_element_type.79
  409.4 9.1 %convolution_bitcast_fusion.1 = f32[2,64,4,128]{3,1,2,0:T(8,128)S(1)} fusion(f32[4,16,64,128,1]{3,2,1,0,4:T(8,128)S(1)} %reshape.318, f32[2,64,4,16,64]{1,4,3,2,0:T(8,128)} %copy.335, f32[2,64,4,16]{1,3,2,0:T(8,128)S(1)} %copy-done.39), kind=kOutput, calls=%fused_computation.108 | convolution fusion | flops 805830656 | bytes 4489216 | tf_op jit(solution)/shard_map/transpose(jvp(ctgn,grpn->ctgrp))/dot_general | solution.py:105
  418.5 8.9 %fusion.70 = f32[2,4,64,128]{3,2,1,0:T(8,128)S(1)} fusion(f32[2,4,16,64,128]{4,3,2,1,0:T(8,128)} %get-tuple-element.578, f32[2,64,4,16,64]{1,4,3,2,0:T(8,128)S(1)} %copy-done.1, f32[2,64,4,16]{1,3,2,0:T(8,128)S(1)} %get-tuple-element.358), kind=kOutput, calls=%fused_computation.105 | convolution fusion | flops 805830656 | bytes 6586368 | tf_op jit(solution)/shard_map/transpose(jvp(ctgn,cgrpn->ctgrp))/dot_general | solution.py:97
  428.7 5.5 fusion.13
  436.3 4.1 copy.348
  444.6 10.6 %while.39 = (s32[]{:T(128)}, f32[4,16]{1,0:T(4,128)S(1)}, f32[4,16,64,128]{3,2,1,0:T(8,128)S(1)}, f32[2,4,16]{2,1,0:T(4,128)S(1)}, f32[2,4,16,64,128]{4,3,2,1,0:...) while((s32[]{:T(128)}, f32[4,16]{1,0:T(4,128)S(1)}, ...), condition=%wide.region_12.13_spmd, body=%wide.region_10.12_spmd.sunk | while | flops 2097347 | bytes 29370552 | solution.py:78
  455.3 7.9 %fusion.11 = (f32[2,64,4,16]{1,3,2,0:T(8,128)}, f32[2,4,16,64,64]{4,3,2,1,0:T(8,128)S(1)}) fusion(f32[2,64,4,16,64]{1,4,3,2,0:T(8,128)} %copy.322, f32[2,4,16,64,128]{4,3,2,1,0:T(8,128)} %get-tuple-element.274, f32[2,64,4,128,1]{3,2,1,0,4:T(4,128)S(1)} %bitcast.333), kind=kOutput, calls=%fused_computation.27 | convolution fusion | flops 806346752 | bytes 8683520 | tf_op jit(solution)/shard_map/transpose(jvp(cqgrp,cqgn->cgrpn))/dot_general | solution.py:68
  463.2 7.9 %fusion.67 = f32[2,64,4,128]{3,1,2,0:T(8,128)} fusion(f32[2,4,16,64,128]{4,3,2,1,0:T(8,128)S(1)} %copy-done.12, f32[2,64,4,16,64]{1,4,3,2,0:T(8,128)S(1)} %copy-done.7, f32[2,64,4,16]{1,3,2,0:T(8,128)S(1)} %copy-done.37), kind=kOutput, calls=%fused_computation.104 | convolution fusion | flops 805830656 | bytes 6586368 | tf_op jit(solution)/shard_map/transpose(jvp(cqgrp,cqgn->cgrpn))/dot_general | solution.py:68
  471.1 5.8 fusion.10
  476.9 6.3 %copy.357 = f32[2,64,4,16,64]{4,3,2,1,0:T(8,128)} copy(f32[2,64,4,16,64]{1,4,3,2,0:T(8,128)} %fusion.10) | data formatting | bytes 4194304 | tf_op jit(solution)/shard_map/add | solution.py:221
  483.1 4.9 reshape.305
  491.1 5.0 multiply_reduce_fusion.4
  502.8 3.2 collective-permute-start.1
  513.2 24.6 %psum.15 = f32[3,64]{1,0:T(4,128)S(1)} all-reduce(f32[3,64]{1,0:T(4,128)S(1)} %pad_maximum_fusion.8), channel_id=1, replica_groups=mesh['groups'=2,'ctx'=16] {'ctx'}, use_global_device_ids=true, to_apply=%region_30.31 | all-reduce | flops 192 | bytes 1536 | tf_op jit(solution)/shard_map/psum | solution.py:235
  541.2 59.6 %all-reduce.33.cloned.1.call-done = f32[5,5120]{1,0:T(8,128)} async-done(((f32[5,5120]{1,0:T(8,128)}), f32[5,5120]{1,0:T(8,128)}) %all-reduce.33.cloned.1.call-update) | async-done | bytes 102416 | tf_op jit(solution)/shard_map/psum | solution.py:235
  (369 shorter events, 156.1 us)
Async XLA Ops:
  7.2 11.1 %copy-start.35 = (bf16[128,5120]{1,0:T(8,128)(2,1)S(1)}, bf16[128,5120]{1,0:T(8,128)(2,1)}, u32[]{:S(2)}) copy-start(bf16[128,5120]{1,0:T(8,128)(2,1)} %param.13) | copy-start | bytes 3932164
  8.8 9.4 %collective-permute-start = (bf16[3,5120]{1,0:T(4,128)(2,1)}, bf16[3,5120]{1,0:T(4,128)(2,1)}, u32[]{:S(2)}, u32[]{:S(2)}) collective-permute-start(bf16[3,5120]{1,0:T(4,128)(2,1)} %slice.256), channel_id=1, source_target_pairs={{0,1},{1,2},{2,3},{3,4},{4,5},{5,6},{6,7},{7,8},{8,9},{9,10},{10,1... | collective-permute-start | bytes 92168 | tf_op jit(solution)/shard_map/ppermute | solution.py:15
  12.4 7.0 %copy-start.72 = (f32[128]{0:T(128)}, f32[128]{0:T(128)S(1)}, u32[]{:S(2)}) copy-start(f32[128]{0:T(128)S(1)} %get-tuple-element.361) | copy-start | bytes 1540
  17.3 5.3 copy-start.50
  17.3 5.3 copy-start.52
  17.6 19.7 %copy-start.36 = (f32[2,64,4,16]{1,3,2,0:T(8,128)}, f32[2,64,4,16]{1,3,2,0:T(8,128)S(1)}, u32[]{:S(2)}) copy-start(f32[2,64,4,16]{1,3,2,0:T(8,128)S(1)} %copy_multiply_fusion) | copy-start | bytes 98308
  53.4 6.9 %copy-start.61 = (f32[2,4,16,1,1]{2,1,4,3,0:T(4,128)}, f32[2,4,16,1,1]{2,1,4,3,0:T(4,128)S(1)}, u32[]{:S(2)}) copy-start(f32[2,4,16,1,1]{2,1,4,3,0:T(4,128)S(1)} %get-tuple-element.577) | copy-start | bytes 1540
  76.0 11.5 %all-to-all-start.1 = ((f32[64,16,1]{0,2,1:T(1,128)}), f32[64,16,1]{0,2,1:T(1,128)S(1)}, u32[]{:S(2)}, u32[]{:S(2)}) async-start(f32[64,16,1]{0,2,1:T(1,128)} %broadcast_in_dim.115), calls=%async_computation.1 | async-start | bytes 16384 | tf_op jit(solution)/shard_map/all_to_all | solution.py:189
  87.4 51.4 %all-to-all-start = ((f32[16,64,1,512]{3,1,2,0:T(8,128)}), f32[16,64,1,512]{3,1,2,0:T(8,128)S(1)}, u32[]{:S(2)}, u32[]{:S(2)}) async-start(f32[16,64,1,512]{3,1,2,0:T(8,128)} %copy.330), calls=%async_computation | async-start | bytes 4194304 | tf_op jit(solution)/shard_map/all_to_all | solution.py:184
  140.9 8.5 %copy-start.80 = (f32[64,3,1]{0,1,2:T(4,128)S(1)}, f32[64,3,1]{0,1,2:T(4,128)}, u32[]{:S(2)}) copy-start(f32[64,3,1]{0,1,2:T(4,128)} %copy.453) | copy-start | bytes 2308
  144.9 10.7 %slice-start.1 = ((f32[64,8,512]{2,0,1:T(8,128)}), f32[64,1,512]{2,0,1:T(8,128)S(1)}, s32[]{:S(2)}) async-start(f32[64,8,512]{2,0,1:T(8,128)} %copy-done.26), calls=%async_computation.7 | async-start | bytes 262144 | tf_op jit(solution)/shard_map/slice | solution.py:118
  157.4 7.0 %copy-start.68 = (f32[64,7,1]{0,1,2:T(8,128)S(1)}, f32[64,7,1]{0,1,2:T(8,128)}, u32[]{:S(2)}) copy-start(f32[64,7,1]{0,1,2:T(8,128)} %copy.451) | copy-start | bytes 5380
  176.9 52.3 %all-to-all-start.2 = ((f32[64,16,512]{2,0,1:T(8,128)}), f32[64,16,512]{2,0,1:T(8,128)S(1)}, u32[]{:S(2)}, u32[]{:S(2)}) async-start(f32[64,16,512]{2,0,1:T(8,128)} %concatenate.38), calls=%async_computation.2 | async-start | bytes 4194304 | tf_op jit(solution)/shard_map/all_to_all | solution.py:193
  186.6 5.9 copy-start.42
  238.4 10.1 %copy-start.13 = (f32[4,16,64,2,64]{4,2,1,0,3:T(8,128)}, f32[4,16,64,2,64]{4,2,1,0,3:T(8,128)S(1)}, u32[]{:S(2)}) copy-start(f32[4,16,64,2,64]{4,2,1,0,3:T(8,128)S(1)} %fusion.90) | copy-start | bytes 6291460
  238.4 10.0 %copy-start.31 = (f32[2,64,4,16]{1,3,2,0:T(8,128)S(1)}, f32[2,64,4,16]{1,3,2,0:T(8,128)}, u32[]{:S(2)}) copy-start(f32[2,64,4,16]{1,3,2,0:T(8,128)} %copy-done.30) | copy-start | bytes 98308
  238.4 10.0 %copy-start.70 = (f32[2,64]{1,0:T(2,128)S(1)}, f32[2,64]{1,0:T(2,128)}, u32[]{:S(2)}) copy-start(f32[2,64]{1,0:T(2,128)} %get-tuple-element.405) | copy-start | bytes 1540
  261.2 6.6 %copy-start.60 = (f32[64,8,1]{0,2,1:T(1,128)S(1)}, f32[64,8,1]{0,2,1:T(1,128)}, u32[]{:S(2)}) copy-start(f32[64,8,1]{0,2,1:T(1,128)} %get-tuple-element.394) | copy-start | bytes 6148
  261.2 6.6 %copy-start.69 = (f32[64,7,1]{0,2,1:T(1,128)S(1)}, f32[64,7,1]{0,2,1:T(1,128)}, u32[]{:S(2)}) copy-start(f32[64,7,1]{0,2,1:T(1,128)} %get-tuple-element.392) | copy-start | bytes 5380
  261.2 52.5 %all-to-all-start.3 = ((f32[64,16,512]{2,0,1:T(8,128)}), f32[64,16,512]{2,0,1:T(8,128)}, u32[]{:S(2)}, u32[]{:S(2)}) async-start(f32[64,16,512]{2,0,1:T(8,128)} %copy.347), calls=%async_computation.3 | async-start | bytes 4194304 | tf_op jit(solution)/shard_map/all_to_all | solution.py:207
  319.4 10.5 %slice-start = ((f32[64,8,512]{2,0,1:T(8,128)}), f32[64,1,512]{2,0,1:T(8,128)S(1)}, s32[]{:S(2)}) async-start(f32[64,8,512]{2,0,1:T(8,128)} %copy-done.25), calls=%async_computation.6 | async-start | bytes 262144 | tf_op jit(solution)/shard_map/slice | solution.py:118
  362.6 71.7 %all-to-all-start.4 = ((f32[64,16,512]{2,0,1:T(8,128)}), f32[64,16,512]{2,0,1:T(8,128)}, u32[]{:S(2)}, u32[]{:S(2)}) async-start(f32[64,16,512]{2,0,1:T(8,128)} %concatenate.42), calls=%async_computation.4 | async-start | bytes 4194304 | tf_op jit(solution)/shard_map/all_to_all | solution.py:212
  369.2 231.7 %all-reduce.33.cloned.1.call-start = ((), (), s32[]{:S(2)}) async-start(), calls=%async_computation.5 | async-start | bytes 327680 | tf_op jit(solution)/shard_map/psum | solution.py:235
  380.2 9.7 %copy-start.6 = (f32[2,64,4,16,64]{1,4,3,2,0:T(8,128)S(1)}, f32[2,64,4,16,64]{1,4,3,2,0:T(8,128)}, u32[]{:S(2)}) copy-start(f32[2,64,4,16,64]{1,4,3,2,0:T(8,128)} %copy.322) | copy-start | bytes 6291460
  380.2 9.7 %copy-start.14 = (f32[4,16,64,2,64]{4,2,1,0,3:T(8,128)S(1)}, f32[4,16,64,2,64]{4,2,1,0,3:T(8,128)}, u32[]{:S(2)}) copy-start(f32[4,16,64,2,64]{4,2,1,0,3:T(8,128)} %copy-done.13) | copy-start | bytes 6291460
  380.2 9.7 %copy-start.17 = (f32[2,4,16,64,64]{4,3,2,1,0:T(8,128)S(1)}, f32[2,4,16,64,64]{4,3,2,1,0:T(8,128)}, u32[]{:S(2)}) copy-start(f32[2,4,16,64,64]{4,3,2,1,0:T(8,128)} %get-tuple-element.410) | copy-start | bytes 6291460
  380.2 9.7 %copy-start.39 = (f32[2,64,4,16]{1,3,2,0:T(8,128)S(1)}, f32[2,64,4,16]{1,3,2,0:T(8,128)}, u32[]{:S(2)}) copy-start(f32[2,64,4,16]{1,3,2,0:T(8,128)} %copy-done.38) | copy-start | bytes 98308
  409.3 9.2 %copy-start.1 = (f32[2,64,4,16,64]{1,4,3,2,0:T(8,128)S(1)}, f32[2,64,4,16,64]{1,4,3,2,0:T(8,128)}, u32[]{:S(2)}) copy-start(f32[2,64,4,16,64]{1,4,3,2,0:T(8,128)} %copy.335) | copy-start | bytes 6291460
  418.5 8.9 %copy-start.40 = (f32[2,4,64,64]{3,2,1,0:T(8,128)S(1)}, f32[2,4,64,64]{3,2,1,0:T(8,128)}, u32[]{:S(2)}) copy-start(f32[2,4,64,64]{3,2,1,0:T(8,128)} %get-tuple-element.310) | copy-start | bytes 393220
  428.7 5.6 copy-start.16
  455.2 8.0 %copy-start.7 = (f32[2,64,4,16,64]{1,4,3,2,0:T(8,128)S(1)}, f32[2,64,4,16,64]{1,4,3,2,0:T(8,128)}, u32[]{:S(2)}) copy-start(f32[2,64,4,16,64]{1,4,3,2,0:T(8,128)} %copy.322) | copy-start | bytes 6291460
  455.2 8.0 %copy-start.12 = (f32[2,4,16,64,128]{4,3,2,1,0:T(8,128)S(1)}, f32[2,4,16,64,128]{4,3,2,1,0:T(8,128)}, u32[]{:S(2)}) copy-start(f32[2,4,16,64,128]{4,3,2,1,0:T(8,128)} %get-tuple-element.274) | copy-start | bytes 12582916
  455.2 8.0 %copy-start.37 = (f32[2,64,4,16]{1,3,2,0:T(8,128)S(1)}, f32[2,64,4,16]{1,3,2,0:T(8,128)}, u32[]{:S(2)}) copy-start(f32[2,64,4,16]{1,3,2,0:T(8,128)} %copy-done.36) | copy-start | bytes 98308
  463.2 7.9 %copy-start.2 = (f32[2,64,4,16,64]{1,4,3,2,0:T(8,128)S(1)}, f32[2,64,4,16,64]{1,4,3,2,0:T(8,128)}, u32[]{:S(2)}) copy-start(f32[2,64,4,16,64]{1,4,3,2,0:T(8,128)} %copy.335) | copy-start | bytes 6291460
  463.2 7.9 %copy-start.24 = (bf16[2,64,4,16,64]{1,4,3,2,0:T(8,128)(2,1)S(1)}, bf16[2,64,4,16,64]{1,4,3,2,0:T(8,128)(2,1)}, u32[]{:S(2)}) copy-start(bf16[2,64,4,16,64]{1,4,3,2,0:T(8,128)(2,1)} %copy.337) | copy-start | bytes 3145732
  483.1 7.8 %copy-start.4 = (f32[131,5120]{1,0:T(8,128)S(1)}, f32[131,5120]{1,0:T(8,128)}, u32[]{:S(2)}) copy-start(f32[131,5120]{1,0:T(8,128)} %copy-done.3) | copy-start | bytes 8048644
  500.5 5.6 copy-start.85
  500.5 6.5 %copy-start.34 = (f32[2,64,4,16]{1,0,3,2:T(2,128)S(1)}, f32[2,64,4,16]{1,0,3,2:T(2,128)}, u32[]{:S(2)}) copy-start(f32[2,64,4,16]{1,0,3,2:T(2,128)} %copy-done.32) | copy-start | bytes 98308
  500.5 6.5 %copy-start.45 = (f32[2,64,4,16]{1,3,2,0:T(8,128)S(1)}, f32[2,64,4,16]{1,3,2,0:T(8,128)}, u32[]{:S(2)}) copy-start(f32[2,64,4,16]{1,3,2,0:T(8,128)} %get-tuple-element.411) | copy-start | bytes 98308
  500.5 6.5 %copy-start.59 = (f32[2,4,16]{2,1,0:T(4,128)S(1)}, f32[2,4,16]{2,1,0:T(4,128)}, u32[]{:S(2)}) copy-start(f32[2,4,16]{2,1,0:T(4,128)} %copy-done.58) | copy-start | bytes 1540
  500.5 6.5 %copy-start.65 = (f32[2,64]{1,0:T(2,128)S(1)}, f32[2,64]{1,0:T(2,128)}, u32[]{:S(2)}) copy-start(f32[2,64]{1,0:T(2,128)} %copy-done.64) | copy-start | bytes 1540
  500.5 6.8 %copy-start.44 = (f32[2,64,4,16]{1,3,2,0:T(8,128)S(1)}, f32[2,64,4,16]{1,3,2,0:T(8,128)}, u32[]{:S(2)}) copy-start(f32[2,64,4,16]{1,3,2,0:T(8,128)} %copy-done.43) | copy-start | bytes 98308
  500.5 6.8 %copy-start.47 = (f32[2,64,4,16]{1,3,2,0:T(8,128)S(1)}, f32[2,64,4,16]{1,3,2,0:T(8,128)}, u32[]{:S(2)}) copy-start(f32[2,64,4,16]{1,3,2,0:T(8,128)} %get-tuple-element.311) | copy-start | bytes 98308
  500.6 6.8 %copy-start.71 = (f32[2,64]{1,0:T(2,128)S(1)}, f32[2,64]{1,0:T(2,128)}, u32[]{:S(2)}) copy-start(f32[2,64]{1,0:T(2,128)} %get-tuple-element.405) | copy-start | bytes 1540
  502.8 8.2 %copy-start.56 = (f32[128,64]{0,1:T(8,128)S(1)}, f32[128,64]{0,1:T(8,128)}, u32[]{:S(2)}) copy-start(f32[128,64]{0,1:T(8,128)} %param.14) | copy-start | bytes 98308
  502.8 8.2 %copy-start.81 = (f32[64]{0:T(128)S(1)}, f32[64]{0:T(128)}, u32[]{:S(2)}) copy-start(f32[64]{0:T(128)} %param.15) | copy-start | bytes 772
  502.8 8.2 %copy-start.83 = (f32[64]{0:T(128)S(1)}, f32[64]{0:T(128)}, u32[]{:S(2)}) copy-start(f32[64]{0:T(128)} %copy-done.82) | copy-start | bytes 772
  502.8 99.6 %collective-permute-start.1 = (f32[3,5120]{1,0:T(4,128)S(1)}, f32[3,5120]{1,0:T(4,128)S(1)}, u32[]{:S(2)}, u32[]{:S(2)}) collective-permute-start(f32[3,5120]{1,0:T(4,128)S(1)} %pad_add_fusion.3), channel_id=1, source_target_pairs={{1,0},{2,1},{3,2},{4,3},{5,4},{6,5},{7,6},{8,7},{9,8},{10,9},{11,1... | collective-permute-start | bytes 184328 | tf_op jit(solution)/shard_map/ppermute | solution.py:15
  (51 other events, 156.0 us)
Sparse Core Ops, SparseCore 0:
  511.2 89.6 all-reduce.32
